TPU v7x, 32 devices: a whole 2x2x4 slice. The times are simulated.
32 devices in a mesh: dp: 8 (over y, x, core), mp: 4 (over z).
Axes of the slice: x: 2, y: 2, z: 4, core: 2. Of those that a mesh axis runs over, the one named last changes fastest.
Arguments:
- buffer: bfloat16 [65536, 256], P(('dp', 'mp')), may hold values from -24 to 24, as said below
- owner: int32 [32768, 1], P(('dp', 'mp')), may hold values from 0 to 31; in each aligned block of 1024 rows (0 to 1023, 1024 to 2047, ...) at most 128 rows name the same one
- local_row: int32 [32768], P(('dp', 'mp')), may hold values from 0 to 2047
- q_in: bfloat16 [2, 130, 256], replicated, may hold values from -0.5 to 0.5
- q_mid: bfloat16 [2, 256, 256], replicated, may hold values from -0.5 to 0.5
- q_out: bfloat16 [2, 256], replicated, may hold values from -0.5 to 0.5
- v_in: bfloat16 [124, 256], replicated, may hold values from -0.5 to 0.5
- v_mid: bfloat16 [256, 256], replicated, may hold values from -0.5 to 0.5
- v_out: bfloat16 [256], replicated, may hold values from -0.5 to 0.5
Outputs:
- q_values: float32 [2, 32768], P(None, ('dp', 'mp'))
- values: float32 [2, 32768], P(None, ('dp', 'mp'))
- targets: float32 [32768], P(('dp', 'mp'))
- q_loss: float32 [32768], P(('dp', 'mp'))
- value_loss: float32 [32768], P(('dp', 'mp'))
Inputs may be any that keep to these rules, and one draw needn't show every extreme that they name: Owner o is the replay owner at position o of the devices in dp+mp order. In the rows of one reader no owner is named more than 128 times, a bound that some block reaches. `buffer`: action values lie in -1 to 1 and discounts in 0 to 0.99.
All inputs are finite; a program needn't handle non-finite values.
Results may differ from a plain program's by a relative error of at most 0.005.
Values may be sent and summed in bfloat16 or wider, within the bound.
A program may use at most 64 MiB of HBM per device.

v0:
```python
import jax
import jax.numpy as jnp
from jax import lax
from jax.sharding import PartitionSpec as P


def layer_two(first, mid, out):
    hidden = jnp.maximum(jnp.dot(first, mid, preferred_element_type=jnp.float32), 0.0)
    return jnp.dot(hidden, out.astype(jnp.float32), precision=lax.Precision.HIGHEST)


def critic_block(rows, weights, states_width, pair_width):
    q_in, q_mid, q_out, v_in, v_mid, v_out = weights
    pair = rows[:, :pair_width]
    state = rows[:, :states_width]
    nexts = rows[:, pair_width : pair_width + states_width]
    reward = rows[:, pair_width + states_width].astype(jnp.float32)
    discount = rows[:, pair_width + states_width + 1].astype(jnp.float32)
    first_one = jnp.maximum(jnp.dot(pair, q_in[0], preferred_element_type=jnp.float32), 0.0).astype(
        jnp.bfloat16
    )
    first_two = jnp.maximum(jnp.dot(pair, q_in[1], preferred_element_type=jnp.float32), 0.0).astype(
        jnp.bfloat16
    )
    q_first = layer_two(first_one, q_mid[0], q_out[0])
    q_second = layer_two(first_two, q_mid[1], q_out[1])
    both = jnp.concatenate([state, nexts], axis=0)
    first_value = jnp.maximum(jnp.dot(both, v_in, preferred_element_type=jnp.float32), 0.0).astype(
        jnp.bfloat16
    )
    value_all = layer_two(first_value, v_mid, v_out)
    count = state.shape[0]
    value_now = value_all[:count]
    value_next = value_all[count:]
    targets = reward + discount * value_next
    return (q_first, q_second, value_now, value_next, targets)


def body(buffer, owner, local_row, q_in, q_mid, q_out, v_in, v_mid, v_out):
    outer = lax.axis_size("dp")
    inner = lax.axis_size("mp")
    owners = outer * inner
    batch = local_row.shape[0]
    columns_all = buffer.shape[1]
    states_width = v_in.shape[0]
    pair_width = q_in.shape[1]
    weights = (q_in, q_mid, q_out, v_in, v_mid, v_out)
    slots_each = max(2, 4 * batch // owners)
    target_owner = owner[:, 0]
    positions = jnp.arange(batch, dtype=jnp.int32)
    same_owner = target_owner[:, None] == target_owner[None, :]
    earlier = positions[None, :] < positions[:, None]
    placed = jnp.sum(jnp.logical_and(same_owner, earlier).astype(jnp.int32), axis=1)
    owner_hot = (target_owner[:, None] == jnp.arange(owners, dtype=jnp.int32)[None, :]).astype(
        jnp.float32
    )
    place_hot = (placed[:, None] == jnp.arange(slots_each, dtype=jnp.int32)[None, :]).astype(
        jnp.float32
    )
    weighted = place_hot * (local_row.astype(jnp.float32) + 1.0)[:, None]
    table = jnp.dot(owner_hot.T, weighted, precision=lax.Precision.HIGHEST)
    requests = (table.astype(jnp.int32) - 1).reshape(outer, inner, slots_each)
    asked = lax.all_to_all(
        lax.all_to_all(requests, "dp", split_axis=0, concat_axis=0, tiled=True),
        "mp",
        split_axis=1,
        concat_axis=1,
        tiled=True,
    )
    picked = jnp.take(buffer, jnp.maximum(asked, 0).reshape(-1), axis=0)

    def evaluate(block):
        return jnp.stack(critic_block(block, weights, states_width, pair_width))

    served = lax.map(evaluate, picked.reshape(outer, inner * slots_each, columns_all))
    served = served.reshape(outer, 5, inner, slots_each)
    returned = lax.all_to_all(
        lax.all_to_all(served, "dp", split_axis=0, concat_axis=0, tiled=True),
        "mp",
        split_axis=2,
        concat_axis=2,
        tiled=True,
    )
    flat = jnp.transpose(returned, (1, 0, 2, 3)).reshape(5, owners, slots_each)
    by_slot = jnp.einsum("kos,bs->kob", flat, place_hot, precision=lax.Precision.HIGHEST)
    mine = jnp.einsum("kob,bo->kb", by_slot, owner_hot, precision=lax.Precision.HIGHEST)
    q_first, q_second, value_now, value_next, targets = (
        mine[0],
        mine[1],
        mine[2],
        mine[3],
        mine[4],
    )
    q_loss = (q_first - targets) ** 2 + (q_second - targets) ** 2
    gap = jnp.minimum(q_first, q_second) - value_now
    value_loss = jnp.where(gap < 0.0, 0.3, 0.7) * gap * gap
    return (
        jnp.stack([q_first, q_second]),
        jnp.stack([value_now, value_next]),
        targets,
        q_loss,
        value_loss,
    )


def solution(mesh):
    return jax.shard_map(
        body,
        mesh=mesh,
        in_specs=(
            P(("dp", "mp"), None),
            P(("dp", "mp"), None),
            P(("dp", "mp")),
            P(),
            P(),
            P(),
            P(),
            P(),
            P(),
        ),
        out_specs=(
            P(None, ("dp", "mp")),
            P(None, ("dp", "mp")),
            P(("dp", "mp")),
            P(("dp", "mp")),
            P(("dp", "mp")),
        ),
        check_vma=False,
    )
```

profile of v0, /device:TPU:0, one launch (start us, length us, event | category | flops | bytes accessed | tf_op | source)
XLA Modules:
  0.0 118.4 jit_solution(8527828568259253387)
XLA Ops:
  0.6 1.3 %convert_reduce_fusion = s32[1024]{0:T(1024)S(1)} fusion(s32[1024]{0:T(1024)} %bitcast.125), kind=kLoop, calls=%fused_computation.40 | loop fusion | flops 5241856 | bytes 8192 | tf_op jit(solution)/shard_map/reduce_sum | solution.py:53
  2.7 1.7 %fusion.42 = s32[32,128]{1,0:T(8,128)S(1)} fusion(f32[1024]{0:T(1024)S(1)} %convert_add_fusion, s32[1024]{0:T(1024)S(1)} %convert_reduce_fusion, s32[1024]{0:T(1024)} %bitcast.126), kind=kOutput, calls=%fused_computation.48 | convolution fusion | flops 50634752 | bytes 28672 | tf_op jit(solution)/shard_map/dot_general | solution.py:61
  4.4 9.8 %all_to_all.20 = s32[8,4,128]{2,1,0:T(4,128)S(1)} all-to-all(s32[8,4,128]{2,1,0:T(4,128)S(1)} %bitcast.119), channel_id=1, replica_groups=mesh['dp'=8,'mp'=4] {'dp'}, dimensions={0} | all-to-all | bytes 32768 | tf_op jit(solution)/shard_map/all_to_all | solution.py:64
  14.8 4.9 %all-to-all-start.1 = ((s32[8,4,128]{2,0,1:T(8,128)}), s32[8,4,128]{2,0,1:T(8,128)S(1)}, u32[]{:S(2)}, u32[]{:S(2)}) async-start(s32[8,4,128]{2,0,1:T(8,128)} %copy.41), calls=%async_computation.1 | async-start | bytes 32768 | tf_op jit(solution)/shard_map/all_to_all | solution.py:63
  20.6 4.7 %all-to-all-done.1 = s32[8,4,128]{2,0,1:T(8,128)S(1)} async-done(((s32[8,4,128]{2,0,1:T(8,128)}), s32[8,4,128]{2,0,1:T(8,128)S(1)}, u32[]{:S(2)}, u32[]{:S(2)}) %all-to-all-start.1) | async-done | bytes 16416 | tf_op jit(solution)/shard_map/all_to_all | solution.py:63
  25.3 16.9 %gather_fusion = bf16[4096,256]{1,0:T(8,128)(2,1)} fusion(bf16[2048,256]{1,0:T(8,128)(2,1)S(1)} %copy-done, s32[4096]{0:T(1024)S(1)} %broadcast_clamp_fusion), kind=kCustom, calls=%fused_computation | custom fusion | bytes 4210688 | tf_op jit(solution)/shard_map/jit(_take)/gather | solution.py:70
  42.3 2.9 %copy.43 = bf16[8,512,256]{1,2,0:T(8,128)(2,1)S(1)} copy(bf16[8,512,256]{2,1,0:T(8,128)(2,1)} %bitcast.104) | data formatting | bytes 4194304 | tf_op jit(solution)/shard_map/jit(_take)/gather | solution.py:70
  45.2 1.5 %broadcast_select_fusion = bf16[8,512,256]{1,2,0:T(8,128)(2,1)} fusion(bf16[8,512,256]{1,2,0:T(8,128)(2,1)S(1)} %copy.43, pred[8,512]{1,0:T(8,128)(4,1)S(1)} %compare_and_fusion), kind=kLoop, calls=%fused_computation.43 | loop fusion | flops 1048576 | bytes 4198400 | tf_op jit(solution)/shard_map/jit(_take)/select_n | solution.py:70
  46.7 51.7 %while.10 = (s32[]{:T(128)}, f32[8,5,512]{2,0,1:T(8,128)}, bf16[8,512,256]{1,2,0:T(8,128)(2,1)}, bf16[2,130,256]{2,1,0:T(8,128)(2,1)S(1)}, bf16[2,256,256]{2,1,0...) while((s32[]{:T(128)}, f32[8,5,512]{2,0,1:T(8,128)}, ...), condition=%wide.region_2.3_spmd, body=%wide.region_1.2_spmd.sunk | while | flops 409978880 | bytes 7499437 | solution.py:75
  46.7 1.0 dynamic-slice_bitcast_fusion.2
  47.8 1.5 %convolution_maximum_fusion.11 = f32[1024,256]{1,0:T(8,128)S(1)} fusion(bf16[256,256]{1,0:T(8,128)(2,1)} %get-tuple-element.229, bf16[124,256]{1,0:T(8,128)(2,1)} %get-tuple-element.228, bf16[512,124]{0,1:T(8,128)(2,1)S(1)} %get-tuple-element.195, bf16[512,124]{0,1:T(8,128)(2,1)S(1)} %get-tuple-element.196), kind=kOutput, calls=%fused_computation.1.clone.1 | convolution fusion | flops 200523776 | bytes 1497088 | tf_op jit(solution)/shard_map/while/body/eval_jaxpr/dot_general | solution.py:8
  51.6 1.6 %dynamic_update_slice.5 = f32[8,5,512]{2,0,1:T(8,128)} dynamic-update-slice(f32[8,5,512]{2,0,1:T(8,128)} %get-tuple-element.212, f32[1,5,512]{2,0,1:T(1,128)S(1)} %copy.60, s32[]{:T(128)} %get-tuple-element.211, s32[]{:T(128)} %constant.20.clone.1..sunk, s32[]{:T(128)} %constant.20.clone.1..sunk) | dynamic-update-slice | bytes 20484 | tf_op jit(solution)/shard_map/while/body/jit(dynamic_update_index_in_dim)/dynamic_update_slice | solution.py:75
  54.2 1.5 %convolution_maximum_fusion.11 = f32[1024,256]{1,0:T(8,128)S(1)} fusion(bf16[256,256]{1,0:T(8,128)(2,1)} %get-tuple-element.229, bf16[124,256]{1,0:T(8,128)(2,1)} %get-tuple-element.228, bf16[512,124]{0,1:T(8,128)(2,1)S(1)} %get-tuple-element.195, bf16[512,124]{0,1:T(8,128)(2,1)S(1)} %get-tuple-element.196), kind=kOutput, calls=%fused_computation.1.clone.1 | convolution fusion | flops 200523776 | bytes 1497088 | tf_op jit(solution)/shard_map/while/body/eval_jaxpr/dot_general | solution.py:8
  58.1 1.6 %dynamic_update_slice.5 = f32[8,5,512]{2,0,1:T(8,128)} dynamic-update-slice(f32[8,5,512]{2,0,1:T(8,128)} %get-tuple-element.212, f32[1,5,512]{2,0,1:T(1,128)S(1)} %copy.60, s32[]{:T(128)} %get-tuple-element.211, s32[]{:T(128)} %constant.20.clone.1..sunk, s32[]{:T(128)} %constant.20.clone.1..sunk) | dynamic-update-slice | bytes 20484 | tf_op jit(solution)/shard_map/while/body/jit(dynamic_update_index_in_dim)/dynamic_update_slice | solution.py:75
  59.6 1.0 dynamic-slice_bitcast_fusion.2
  60.7 1.5 %convolution_maximum_fusion.11 = f32[1024,256]{1,0:T(8,128)S(1)} fusion(bf16[256,256]{1,0:T(8,128)(2,1)} %get-tuple-element.229, bf16[124,256]{1,0:T(8,128)(2,1)} %get-tuple-element.228, bf16[512,124]{0,1:T(8,128)(2,1)S(1)} %get-tuple-element.195, bf16[512,124]{0,1:T(8,128)(2,1)S(1)} %get-tuple-element.196), kind=kOutput, calls=%fused_computation.1.clone.1 | convolution fusion | flops 200523776 | bytes 1497088 | tf_op jit(solution)/shard_map/while/body/eval_jaxpr/dot_general | solution.py:8
  64.5 1.6 %dynamic_update_slice.5 = f32[8,5,512]{2,0,1:T(8,128)} dynamic-update-slice(f32[8,5,512]{2,0,1:T(8,128)} %get-tuple-element.212, f32[1,5,512]{2,0,1:T(1,128)S(1)} %copy.60, s32[]{:T(128)} %get-tuple-element.211, s32[]{:T(128)} %constant.20.clone.1..sunk, s32[]{:T(128)} %constant.20.clone.1..sunk) | dynamic-update-slice | bytes 20484 | tf_op jit(solution)/shard_map/while/body/jit(dynamic_update_index_in_dim)/dynamic_update_slice | solution.py:75
  66.1 1.0 dynamic-slice_bitcast_fusion.2
  67.2 1.5 %convolution_maximum_fusion.11 = f32[1024,256]{1,0:T(8,128)S(1)} fusion(bf16[256,256]{1,0:T(8,128)(2,1)} %get-tuple-element.229, bf16[124,256]{1,0:T(8,128)(2,1)} %get-tuple-element.228, bf16[512,124]{0,1:T(8,128)(2,1)S(1)} %get-tuple-element.195, bf16[512,124]{0,1:T(8,128)(2,1)S(1)} %get-tuple-element.196), kind=kOutput, calls=%fused_computation.1.clone.1 | convolution fusion | flops 200523776 | bytes 1497088 | tf_op jit(solution)/shard_map/while/body/eval_jaxpr/dot_general | solution.py:8
  71.0 1.6 %dynamic_update_slice.5 = f32[8,5,512]{2,0,1:T(8,128)} dynamic-update-slice(f32[8,5,512]{2,0,1:T(8,128)} %get-tuple-element.212, f32[1,5,512]{2,0,1:T(1,128)S(1)} %copy.60, s32[]{:T(128)} %get-tuple-element.211, s32[]{:T(128)} %constant.20.clone.1..sunk, s32[]{:T(128)} %constant.20.clone.1..sunk) | dynamic-update-slice | bytes 20484 | tf_op jit(solution)/shard_map/while/body/jit(dynamic_update_index_in_dim)/dynamic_update_slice | solution.py:75
  72.6 1.0 dynamic-slice_bitcast_fusion.2
  73.6 1.5 %convolution_maximum_fusion.11 = f32[1024,256]{1,0:T(8,128)S(1)} fusion(bf16[256,256]{1,0:T(8,128)(2,1)} %get-tuple-element.229, bf16[124,256]{1,0:T(8,128)(2,1)} %get-tuple-element.228, bf16[512,124]{0,1:T(8,128)(2,1)S(1)} %get-tuple-element.195, bf16[512,124]{0,1:T(8,128)(2,1)S(1)} %get-tuple-element.196), kind=kOutput, calls=%fused_computation.1.clone.1 | convolution fusion | flops 200523776 | bytes 1497088 | tf_op jit(solution)/shard_map/while/body/eval_jaxpr/dot_general | solution.py:8
  77.5 1.6 %dynamic_update_slice.5 = f32[8,5,512]{2,0,1:T(8,128)} dynamic-update-slice(f32[8,5,512]{2,0,1:T(8,128)} %get-tuple-element.212, f32[1,5,512]{2,0,1:T(1,128)S(1)} %copy.60, s32[]{:T(128)} %get-tuple-element.211, s32[]{:T(128)} %constant.20.clone.1..sunk, s32[]{:T(128)} %constant.20.clone.1..sunk) | dynamic-update-slice | bytes 20484 | tf_op jit(solution)/shard_map/while/body/jit(dynamic_update_index_in_dim)/dynamic_update_slice | solution.py:75
  80.1 1.5 %convolution_maximum_fusion.11 = f32[1024,256]{1,0:T(8,128)S(1)} fusion(bf16[256,256]{1,0:T(8,128)(2,1)} %get-tuple-element.229, bf16[124,256]{1,0:T(8,128)(2,1)} %get-tuple-element.228, bf16[512,124]{0,1:T(8,128)(2,1)S(1)} %get-tuple-element.195, bf16[512,124]{0,1:T(8,128)(2,1)S(1)} %get-tuple-element.196), kind=kOutput, calls=%fused_computation.1.clone.1 | convolution fusion | flops 200523776 | bytes 1497088 | tf_op jit(solution)/shard_map/while/body/eval_jaxpr/dot_general | solution.py:8
  83.9 1.6 %dynamic_update_slice.5 = f32[8,5,512]{2,0,1:T(8,128)} dynamic-update-slice(f32[8,5,512]{2,0,1:T(8,128)} %get-tuple-element.212, f32[1,5,512]{2,0,1:T(1,128)S(1)} %copy.60, s32[]{:T(128)} %get-tuple-element.211, s32[]{:T(128)} %constant.20.clone.1..sunk, s32[]{:T(128)} %constant.20.clone.1..sunk) | dynamic-update-slice | bytes 20484 | tf_op jit(solution)/shard_map/while/body/jit(dynamic_update_index_in_dim)/dynamic_update_slice | solution.py:75
  86.5 1.5 %convolution_maximum_fusion.11 = f32[1024,256]{1,0:T(8,128)S(1)} fusion(bf16[256,256]{1,0:T(8,128)(2,1)} %get-tuple-element.229, bf16[124,256]{1,0:T(8,128)(2,1)} %get-tuple-element.228, bf16[512,124]{0,1:T(8,128)(2,1)S(1)} %get-tuple-element.195, bf16[512,124]{0,1:T(8,128)(2,1)S(1)} %get-tuple-element.196), kind=kOutput, calls=%fused_computation.1.clone.1 | convolution fusion | flops 200523776 | bytes 1497088 | tf_op jit(solution)/shard_map/while/body/eval_jaxpr/dot_general | solution.py:8
  90.4 1.6 %dynamic_update_slice.5 = f32[8,5,512]{2,0,1:T(8,128)} dynamic-update-slice(f32[8,5,512]{2,0,1:T(8,128)} %get-tuple-element.212, f32[1,5,512]{2,0,1:T(1,128)S(1)} %copy.60, s32[]{:T(128)} %get-tuple-element.211, s32[]{:T(128)} %constant.20.clone.1..sunk, s32[]{:T(128)} %constant.20.clone.1..sunk) | dynamic-update-slice | bytes 20484 | tf_op jit(solution)/shard_map/while/body/jit(dynamic_update_index_in_dim)/dynamic_update_slice | solution.py:75
  93.0 1.5 %convolution_maximum_fusion.11 = f32[1024,256]{1,0:T(8,128)S(1)} fusion(bf16[256,256]{1,0:T(8,128)(2,1)} %get-tuple-element.229, bf16[124,256]{1,0:T(8,128)(2,1)} %get-tuple-element.228, bf16[512,124]{0,1:T(8,128)(2,1)S(1)} %get-tuple-element.195, bf16[512,124]{0,1:T(8,128)(2,1)S(1)} %get-tuple-element.196), kind=kOutput, calls=%fused_computation.1.clone.1 | convolution fusion | flops 200523776 | bytes 1497088 | tf_op jit(solution)/shard_map/while/body/eval_jaxpr/dot_general | solution.py:8
  96.8 1.6 %dynamic_update_slice.5 = f32[8,5,512]{2,0,1:T(8,128)} dynamic-update-slice(f32[8,5,512]{2,0,1:T(8,128)} %get-tuple-element.212, f32[1,5,512]{2,0,1:T(1,128)S(1)} %copy.60, s32[]{:T(128)} %get-tuple-element.211, s32[]{:T(128)} %constant.20.clone.1..sunk, s32[]{:T(128)} %constant.20.clone.1..sunk) | dynamic-update-slice | bytes 20484 | tf_op jit(solution)/shard_map/while/body/jit(dynamic_update_index_in_dim)/dynamic_update_slice | solution.py:75
  99.3 7.5 %all_to_all.21 = f32[8,5,4,128]{3,2,1,0:T(4,128)S(1)} all-to-all(f32[8,5,4,128]{3,2,1,0:T(4,128)S(1)} %copy.46), channel_id=1, replica_groups=mesh['dp'=8,'mp'=4] {'dp'}, dimensions={0} | all-to-all | bytes 163840 | tf_op jit(solution)/shard_map/all_to_all | solution.py:78
  107.4 3.3 %all-to-all-start.3 = ((f32[8,5,4,128]{3,0,1,2:T(8,128)}), f32[8,5,4,128]{3,0,1,2:T(8,128)S(1)}, u32[]{:S(2)}, u32[]{:S(2)}) async-start(f32[8,5,4,128]{3,0,1,2:T(8,128)} %copy.47), calls=%async_computation.3 | async-start | bytes 163840 | tf_op jit(solution)/shard_map/all_to_all | solution.py:77
  111.1 5.4 %all-to-all-done.3 = f32[8,5,4,128]{3,0,1,2:T(8,128)S(1)} async-done(((f32[8,5,4,128]{3,0,1,2:T(8,128)}), f32[8,5,4,128]{3,0,1,2:T(8,128)S(1)}, u32[]{:S(2)}, u32[]{:S(2)}) %all-to-all-start.3) | async-done | bytes 81952 | tf_op jit(solution)/shard_map/all_to_all | solution.py:77
  (154 shorter events, 28.6 us)
Async XLA Ops:
  0.6 24.7 %copy-start = (bf16[2048,256]{1,0:T(8,128)(2,1)S(1)}, bf16[2048,256]{1,0:T(8,128)(2,1)}, u32[]{:S(2)}) copy-start(bf16[2048,256]{1,0:T(8,128)(2,1)} %param.11) | copy-start | bytes 3145732
  2.0 2.4 %copy-start.6 = (s32[1024]{0:T(1024)}, s32[1024]{0:T(1024)S(1)}, u32[]{:S(2)}) copy-start(s32[1024]{0:T(1024)S(1)} %convert_reduce_fusion) | copy-start | bytes 12292
  14.8 10.5 %all-to-all-start.1 = ((s32[8,4,128]{2,0,1:T(8,128)}), s32[8,4,128]{2,0,1:T(8,128)S(1)}, u32[]{:S(2)}, u32[]{:S(2)}) async-start(s32[8,4,128]{2,0,1:T(8,128)} %copy.41), calls=%async_computation.1 | async-start | bytes 32768 | tf_op jit(solution)/shard_map/all_to_all | solution.py:63
  45.1 1.5 %copy-start.1 = (bf16[2,256]{1,0:T(2,128)(2,1)S(1)}, bf16[2,256]{1,0:T(2,128)(2,1)}, u32[]{:S(2)}) copy-start(bf16[2,256]{1,0:T(2,128)(2,1)} %param.16) | copy-start | bytes 3076
  46.7 64.0 %copy-start.3 = (s32[1024,1]{0,1:T(1,128)S(1)}, s32[1024,1]{0,1:T(1,128)}, u32[]{:S(2)}) copy-start(s32[1024,1]{0,1:T(1,128)} %param.12) | copy-start | bytes 12292
  46.7 69.8 %copy-start.7 = (s32[1024]{0:T(1024)S(1)}, s32[1024]{0:T(1024)}, u32[]{:S(2)}) copy-start(s32[1024]{0:T(1024)} %copy-done.6) | copy-start | bytes 12292
  46.7 2.6 %copy-start.5 = (bf16[256]{0:T(256)(128)(2,1)S(1)}, bf16[256]{0:T(256)(128)(2,1)}, u32[]{:S(2)}) copy-start(bf16[256]{0:T(256)(128)(2,1)} %get-tuple-element.230) | copy-start | bytes 1540 | tf_op jit(solution)/shard_map/while
  46.7 3.2 %copy-start.4 = (bf16[2,256,256]{2,1,0:T(8,128)(2,1)S(1)}, bf16[2,256,256]{2,1,0:T(8,128)(2,1)}, u32[]{:S(2)}) copy-start(bf16[2,256,256]{2,1,0:T(8,128)(2,1)} %get-tuple-element.226) | copy-start | bytes 786436 | tf_op jit(solution)/shard_map/while
  53.2 2.6 %copy-start.5 = (bf16[256]{0:T(256)(128)(2,1)S(1)}, bf16[256]{0:T(256)(128)(2,1)}, u32[]{:S(2)}) copy-start(bf16[256]{0:T(256)(128)(2,1)} %get-tuple-element.230) | copy-start | bytes 1540 | tf_op jit(solution)/shard_map/while
  53.2 3.2 %copy-start.4 = (bf16[2,256,256]{2,1,0:T(8,128)(2,1)S(1)}, bf16[2,256,256]{2,1,0:T(8,128)(2,1)}, u32[]{:S(2)}) copy-start(bf16[2,256,256]{2,1,0:T(8,128)(2,1)} %get-tuple-element.226) | copy-start | bytes 786436 | tf_op jit(solution)/shard_map/while
  59.6 2.6 %copy-start.5 = (bf16[256]{0:T(256)(128)(2,1)S(1)}, bf16[256]{0:T(256)(128)(2,1)}, u32[]{:S(2)}) copy-start(bf16[256]{0:T(256)(128)(2,1)} %get-tuple-element.230) | copy-start | bytes 1540 | tf_op jit(solution)/shard_map/while
  59.6 3.2 %copy-start.4 = (bf16[2,256,256]{2,1,0:T(8,128)(2,1)S(1)}, bf16[2,256,256]{2,1,0:T(8,128)(2,1)}, u32[]{:S(2)}) copy-start(bf16[2,256,256]{2,1,0:T(8,128)(2,1)} %get-tuple-element.226) | copy-start | bytes 786436 | tf_op jit(solution)/shard_map/while
  66.1 2.6 %copy-start.5 = (bf16[256]{0:T(256)(128)(2,1)S(1)}, bf16[256]{0:T(256)(128)(2,1)}, u32[]{:S(2)}) copy-start(bf16[256]{0:T(256)(128)(2,1)} %get-tuple-element.230) | copy-start | bytes 1540 | tf_op jit(solution)/shard_map/while
  66.1 3.2 %copy-start.4 = (bf16[2,256,256]{2,1,0:T(8,128)(2,1)S(1)}, bf16[2,256,256]{2,1,0:T(8,128)(2,1)}, u32[]{:S(2)}) copy-start(bf16[2,256,256]{2,1,0:T(8,128)(2,1)} %get-tuple-element.226) | copy-start | bytes 786436 | tf_op jit(solution)/shard_map/while
  72.6 2.6 %copy-start.5 = (bf16[256]{0:T(256)(128)(2,1)S(1)}, bf16[256]{0:T(256)(128)(2,1)}, u32[]{:S(2)}) copy-start(bf16[256]{0:T(256)(128)(2,1)} %get-tuple-element.230) | copy-start | bytes 1540 | tf_op jit(solution)/shard_map/while
  72.6 3.2 %copy-start.4 = (bf16[2,256,256]{2,1,0:T(8,128)(2,1)S(1)}, bf16[2,256,256]{2,1,0:T(8,128)(2,1)}, u32[]{:S(2)}) copy-start(bf16[2,256,256]{2,1,0:T(8,128)(2,1)} %get-tuple-element.226) | copy-start | bytes 786436 | tf_op jit(solution)/shard_map/while
  79.0 2.6 %copy-start.5 = (bf16[256]{0:T(256)(128)(2,1)S(1)}, bf16[256]{0:T(256)(128)(2,1)}, u32[]{:S(2)}) copy-start(bf16[256]{0:T(256)(128)(2,1)} %get-tuple-element.230) | copy-start | bytes 1540 | tf_op jit(solution)/shard_map/while
  79.0 3.2 %copy-start.4 = (bf16[2,256,256]{2,1,0:T(8,128)(2,1)S(1)}, bf16[2,256,256]{2,1,0:T(8,128)(2,1)}, u32[]{:S(2)}) copy-start(bf16[2,256,256]{2,1,0:T(8,128)(2,1)} %get-tuple-element.226) | copy-start | bytes 786436 | tf_op jit(solution)/shard_map/while
  85.5 2.6 %copy-start.5 = (bf16[256]{0:T(256)(128)(2,1)S(1)}, bf16[256]{0:T(256)(128)(2,1)}, u32[]{:S(2)}) copy-start(bf16[256]{0:T(256)(128)(2,1)} %get-tuple-element.230) | copy-start | bytes 1540 | tf_op jit(solution)/shard_map/while
  85.5 3.2 %copy-start.4 = (bf16[2,256,256]{2,1,0:T(8,128)(2,1)S(1)}, bf16[2,256,256]{2,1,0:T(8,128)(2,1)}, u32[]{:S(2)}) copy-start(bf16[2,256,256]{2,1,0:T(8,128)(2,1)} %get-tuple-element.226) | copy-start | bytes 786436 | tf_op jit(solution)/shard_map/while
  91.9 2.6 %copy-start.5 = (bf16[256]{0:T(256)(128)(2,1)S(1)}, bf16[256]{0:T(256)(128)(2,1)}, u32[]{:S(2)}) copy-start(bf16[256]{0:T(256)(128)(2,1)} %get-tuple-element.230) | copy-start | bytes 1540 | tf_op jit(solution)/shard_map/while
  91.9 3.2 %copy-start.4 = (bf16[2,256,256]{2,1,0:T(8,128)(2,1)S(1)}, bf16[2,256,256]{2,1,0:T(8,128)(2,1)}, u32[]{:S(2)}) copy-start(bf16[2,256,256]{2,1,0:T(8,128)(2,1)} %get-tuple-element.226) | copy-start | bytes 786436 | tf_op jit(solution)/shard_map/while
  107.4 9.1 %all-to-all-start.3 = ((f32[8,5,4,128]{3,0,1,2:T(8,128)}), f32[8,5,4,128]{3,0,1,2:T(8,128)S(1)}, u32[]{:S(2)}, u32[]{:S(2)}) async-start(f32[8,5,4,128]{3,0,1,2:T(8,128)} %copy.47), calls=%async_computation.3 | async-start | bytes 163840 | tf_op jit(solution)/shard_map/all_to_all | solution.py:77
  117.1 1.2 %copy-start.2 = (f32[1,1024]{1,0:T(1,128)}, f32[1,1024]{1,0:T(1,128)S(1)}, u32[]{:S(2)}) copy-start(f32[1,1024]{1,0:T(1,128)S(1)} %get-tuple-element.126) | copy-start | bytes 12292
where the time goes:
time: 120 us; the launch traced here: 118 us
  local copies, waits for them, and re-layouts  45.1 us (38%)
  matrix products  31.9 us (27%)
  blocking collectives  17.2 us (14%)
  waiting for transfers between devices  10.1 us (8%)
  starting transfers between devices  8.16 us (7%)
  other arithmetic  4.53 us (4%)
    gather x2, local copies, waits for them, and re-layouts, body(): picked = jnp.take(buffer, jnp.maximum(asked, 0).reshape(-1), axis=0)  19.8 us
    dot_general x24, matrix products, layer_two(): jnp.dot(first, mid, preferred_element_type=jnp.float32)  19.4 us
    dynamic_update_slice x16, local copies, waits for them, and re-layouts, body(): lax.map(evaluate, picked.reshape(outer, inner * slots_each, columns_all))  12.5 us
    dot_general x24, matrix products, layer_two(): jnp.dot(hidden, out.astype(jnp.float32), precision=lax.Precision.HIGHEST)  10.2 us
    all_to_all x1, blocking collectives, body(): lax.all_to_all(requests, 'dp', split_axis=0, concat_axis=0, tiled=True)  9.75 us
    squeeze x8, local copies, waits for them, and re-layouts, body(): lax.map(evaluate, picked.reshape(outer, inner * slots_each, columns_all))  8.09 us
    all_to_all x1, blocking collectives, body(): lax.all_to_all(served, 'dp', split_axis=0, concat_axis=0, tiled=True)  7.49 us
    all_to_all x1, waiting for transfers between devices, body(): lax.all_to_all(lax.all_to_all(served, 'dp', split_axis=0, concat_axis=0,...  5.37 us
  transfers between devices with their start and end apart: 2, of which 2 were waited for; matrix products, arithmetic and copies ran while one was open for 1% of the time, Pallas kernels for 0%

commit v1 on v0

--- a/solution.py
+++ b/solution.py
@@ -2,6 +2,12 @@
 import jax.numpy as jnp
 from jax import lax
 from jax.sharding import PartitionSpec as P
+
+
+def stacked_exchange(x, mesh_axis, split, join):
+    shards = jnp.split(x, lax.axis_size(mesh_axis), axis=split)
+    got = lax.all_to_all(jnp.stack(shards), mesh_axis, 0, 0)
+    return jnp.concatenate(got, axis=join)
 
 
 def layer_two(first, mid, out):
@@ -60,12 +66,8 @@
     weighted = place_hot * (local_row.astype(jnp.float32) + 1.0)[:, None]
     table = jnp.dot(owner_hot.T, weighted, precision=lax.Precision.HIGHEST)
     requests = (table.astype(jnp.int32) - 1).reshape(outer, inner, slots_each)
-    asked = lax.all_to_all(
-        lax.all_to_all(requests, "dp", split_axis=0, concat_axis=0, tiled=True),
-        "mp",
-        split_axis=1,
-        concat_axis=1,
-        tiled=True,
+    asked = stacked_exchange(
+        lax.all_to_all(requests, "dp", split_axis=0, concat_axis=0, tiled=True), "mp", 1, 1
     )
     picked = jnp.take(buffer, jnp.maximum(asked, 0).reshape(-1), axis=0)
 

time: 120 us -> 106 us (0.88)
  local copies, waits for them, and re-layouts: 45.1 us -> 31.9 us
    dynamic_update_slice x16, local copies, waits for them, and re-layouts: 12.5 us -> 0.79 us  [body(): lax.map(evaluate, picked.reshape(outer, inner * slots_each, columns_all))]
where the time goes in v1:
time: 106 us; the launch traced here: 105 us
  local copies, waits for them, and re-layouts  31.9 us (30%)
  matrix products  31 us (29%)
  blocking collectives  17.2 us (16%)
  waiting for transfers between devices  10.1 us (10%)
  starting transfers between devices  8.16 us (8%)
  other arithmetic  5.12 us (5%)
    gather x2, local copies, waits for them, and re-layouts, body(): picked = jnp.take(buffer, jnp.maximum(asked, 0).reshape(-1), axis=0)  19.8 us
    dot_general x24, matrix products, layer_two(): jnp.dot(first, mid, preferred_element_type=jnp.float32)  18.5 us
    dot_general x24, matrix products, layer_two(): jnp.dot(hidden, out.astype(jnp.float32), precision=lax.Precision.HIGHEST)  10.2 us
    all_to_all x1, blocking collectives, body(): lax.all_to_all(requests, 'dp', split_axis=0, concat_axis=0, tiled=True)  9.75 us
    squeeze x8, local copies, waits for them, and re-layouts, body(): lax.map(evaluate, picked.reshape(outer, inner * slots_each, columns_all))  8.12 us
    all_to_all x1, blocking collectives, body(): lax.all_to_all(served, 'dp', split_axis=0, concat_axis=0, tiled=True)  7.49 us
    all_to_all x1, waiting for transfers between devices, body(): lax.all_to_all(lax.all_to_all(served, 'dp', split_axis=0, concat_axis=0,...  5.37 us
    all_to_all x1, starting transfers between devices, stacked_exchange(): got = lax.all_to_all(jnp.stack(shards), mesh_axis, 0, 0)  4.87 us
  transfers between devices with their start and end apart: 2, of which 2 were waited for; matrix products, arithmetic and copies ran while one was open for 1% of the time, Pallas kernels for 0%

profile of v1, /device:TPU:0, one launch (start us, length us, event | category | flops | bytes accessed | tf_op | source)
XLA Modules:
  0.0 105.1 jit_solution(4600635458612219945)
XLA Ops:
  0.6 1.3 %convert_reduce_fusion = s32[1024]{0:T(1024)S(1)} fusion(s32[1024]{0:T(1024)} %bitcast.139), kind=kLoop, calls=%fused_computation.40 | loop fusion | flops 5241856 | bytes 8192 | tf_op jit(solution)/shard_map/reduce_sum | solution.py:59
  2.0 0.7 convert_add_fusion
  2.6 1.7 %fusion.42 = s32[32,128]{1,0:T(8,128)S(1)} fusion(f32[1024]{0:T(1024)S(1)} %convert_add_fusion, s32[1024]{0:T(1024)S(1)} %convert_reduce_fusion, s32[1024]{0:T(1024)} %bitcast.140), kind=kOutput, calls=%fused_computation.48 | convolution fusion | flops 50634752 | bytes 28672 | tf_op jit(solution)/shard_map/dot_general | solution.py:67
  4.4 9.8 %all_to_all.20 = s32[8,4,128]{2,1,0:T(4,128)S(1)} all-to-all(s32[8,4,128]{2,1,0:T(4,128)S(1)} %bitcast.129), channel_id=1, replica_groups=mesh['dp'=8,'mp'=4] {'dp'}, dimensions={0} | all-to-all | bytes 32768 | tf_op jit(solution)/shard_map/all_to_all | solution.py:70
  14.8 4.9 %all-to-all-start.1 = ((s32[4,8,1,128]{3,1,2,0:T(8,128)}), s32[4,8,1,128]{3,1,2,0:T(8,128)S(1)}, u32[]{:S(2)}, u32[]{:S(2)}) async-start(s32[4,8,1,128]{3,1,2,0:T(8,128)} %pad_add_fusion), calls=%async_computation.1 | async-start | bytes 32768 | tf_op jit(solution)/shard_map/all_to_all | solution.py:9
  19.6 0.9 copy.40
  20.6 4.7 %all-to-all-done.1 = s32[4,8,1,128]{3,1,2,0:T(8,128)S(1)} async-done(((s32[4,8,1,128]{3,1,2,0:T(8,128)}), s32[4,8,1,128]{3,1,2,0:T(8,128)S(1)}, u32[]{:S(2)}, u32[]{:S(2)}) %all-to-all-start.1) | async-done | bytes 16416 | tf_op jit(solution)/shard_map/all_to_all | solution.py:9
  25.3 16.9 %gather_fusion = bf16[4096,256]{1,0:T(8,128)(2,1)} fusion(bf16[2048,256]{1,0:T(8,128)(2,1)S(1)} %copy-done, s32[4096]{0:T(1024)S(1)} %broadcast_clamp_fusion), kind=kCustom, calls=%fused_computation | custom fusion | bytes 4210688 | tf_op jit(solution)/shard_map/jit(_take)/gather | solution.py:72
  42.2 2.9 %copy.39 = bf16[8,512,256]{1,2,0:T(8,128)(2,1)S(1)} copy(bf16[8,512,256]{2,1,0:T(8,128)(2,1)} %bitcast.115) | data formatting | bytes 4194304 | tf_op jit(solution)/shard_map/jit(_take)/gather | solution.py:72
  45.1 1.5 %broadcast_select_fusion = bf16[8,512,256]{1,2,0:T(8,128)(2,1)} fusion(bf16[8,512,256]{1,2,0:T(8,128)(2,1)S(1)} %copy.39, pred[8,512]{1,0:T(8,128)(4,1)S(1)} %compare_bitcast_fusion), kind=kLoop, calls=%fused_computation.43 | loop fusion | flops 1048576 | bytes 4198400 | tf_op jit(solution)/shard_map/jit(_take)/select_n | solution.py:72
  46.7 39.3 %while.10 = (s32[]{:T(128)}, f32[8,5,512]{2,0,1:T(8,128)S(1)}, bf16[8,512,256]{1,2,0:T(8,128)(2,1)}, bf16[2,130,256]{2,1,0:T(8,128)(2,1)S(1)}, bf16[2,256,256]{2...) while((s32[]{:T(128)}, f32[8,5,512]{2,0,1:T(8,128)S(1)}, ...), condition=%wide.region_2.3_spmd, body=%wide.region_1.2_spmd.sunk | while | flops 409978880 | bytes 7497361 | solution.py:77
  46.7 1.0 dynamic-slice_bitcast_fusion.2
  47.8 1.4 %convolution_maximum_fusion.11 = f32[1024,256]{1,0:T(8,128)S(1)} fusion(bf16[256,256]{1,0:T(8,128)(2,1)S(1)} %get-tuple-element.215, bf16[124,256]{1,0:T(8,128)(2,1)} %get-tuple-element.214, bf16[512,124]{0,1:T(8,128)(2,1)S(1)} %get-tuple-element.181, bf16[512,124]{0,1:T(8,128)(2,1)S(1)} %get-tuple-element.182), kind=kOutput, calls=%fused_computation.1.clone.1 | convolution fusion | flops 200523776 | bytes 1497088 | tf_op jit(solution)/shard_map/while/body/eval_jaxpr/dot_general | solution.py:14
  51.6 1.0 dynamic-slice_bitcast_fusion.2
  52.7 1.4 %convolution_maximum_fusion.11 = f32[1024,256]{1,0:T(8,128)S(1)} fusion(bf16[256,256]{1,0:T(8,128)(2,1)S(1)} %get-tuple-element.215, bf16[124,256]{1,0:T(8,128)(2,1)} %get-tuple-element.214, bf16[512,124]{0,1:T(8,128)(2,1)S(1)} %get-tuple-element.181, bf16[512,124]{0,1:T(8,128)(2,1)S(1)} %get-tuple-element.182), kind=kOutput, calls=%fused_computation.1.clone.1 | convolution fusion | flops 200523776 | bytes 1497088 | tf_op jit(solution)/shard_map/while/body/eval_jaxpr/dot_general | solution.py:14
  56.5 1.0 dynamic-slice_bitcast_fusion.2
  57.6 1.4 %convolution_maximum_fusion.11 = f32[1024,256]{1,0:T(8,128)S(1)} fusion(bf16[256,256]{1,0:T(8,128)(2,1)S(1)} %get-tuple-element.215, bf16[124,256]{1,0:T(8,128)(2,1)} %get-tuple-element.214, bf16[512,124]{0,1:T(8,128)(2,1)S(1)} %get-tuple-element.181, bf16[512,124]{0,1:T(8,128)(2,1)S(1)} %get-tuple-element.182), kind=kOutput, calls=%fused_computation.1.clone.1 | convolution fusion | flops 200523776 | bytes 1497088 | tf_op jit(solution)/shard_map/while/body/eval_jaxpr/dot_general | solution.py:14
  61.5 1.0 dynamic-slice_bitcast_fusion.2
  62.5 1.4 %convolution_maximum_fusion.11 = f32[1024,256]{1,0:T(8,128)S(1)} fusion(bf16[256,256]{1,0:T(8,128)(2,1)S(1)} %get-tuple-element.215, bf16[124,256]{1,0:T(8,128)(2,1)} %get-tuple-element.214, bf16[512,124]{0,1:T(8,128)(2,1)S(1)} %get-tuple-element.181, bf16[512,124]{0,1:T(8,128)(2,1)S(1)} %get-tuple-element.182), kind=kOutput, calls=%fused_computation.1.clone.1 | convolution fusion | flops 200523776 | bytes 1497088 | tf_op jit(solution)/shard_map/while/body/eval_jaxpr/dot_general | solution.py:14
  66.4 1.0 dynamic-slice_bitcast_fusion.2
  67.4 1.4 %convolution_maximum_fusion.11 = f32[1024,256]{1,0:T(8,128)S(1)} fusion(bf16[256,256]{1,0:T(8,128)(2,1)S(1)} %get-tuple-element.215, bf16[124,256]{1,0:T(8,128)(2,1)} %get-tuple-element.214, bf16[512,124]{0,1:T(8,128)(2,1)S(1)} %get-tuple-element.181, bf16[512,124]{0,1:T(8,128)(2,1)S(1)} %get-tuple-element.182), kind=kOutput, calls=%fused_computation.1.clone.1 | convolution fusion | flops 200523776 | bytes 1497088 | tf_op jit(solution)/shard_map/while/body/eval_jaxpr/dot_general | solution.py:14
  71.3 1.0 dynamic-slice_bitcast_fusion.2
  72.3 1.4 %convolution_maximum_fusion.11 = f32[1024,256]{1,0:T(8,128)S(1)} fusion(bf16[256,256]{1,0:T(8,128)(2,1)S(1)} %get-tuple-element.215, bf16[124,256]{1,0:T(8,128)(2,1)} %get-tuple-element.214, bf16[512,124]{0,1:T(8,128)(2,1)S(1)} %get-tuple-element.181, bf16[512,124]{0,1:T(8,128)(2,1)S(1)} %get-tuple-element.182), kind=kOutput, calls=%fused_computation.1.clone.1 | convolution fusion | flops 200523776 | bytes 1497088 | tf_op jit(solution)/shard_map/while/body/eval_jaxpr/dot_general | solution.py:14
  76.2 1.0 dynamic-slice_bitcast_fusion.2
  77.2 1.4 %convolution_maximum_fusion.11 = f32[1024,256]{1,0:T(8,128)S(1)} fusion(bf16[256,256]{1,0:T(8,128)(2,1)S(1)} %get-tuple-element.215, bf16[124,256]{1,0:T(8,128)(2,1)} %get-tuple-element.214, bf16[512,124]{0,1:T(8,128)(2,1)S(1)} %get-tuple-element.181, bf16[512,124]{0,1:T(8,128)(2,1)S(1)} %get-tuple-element.182), kind=kOutput, calls=%fused_computation.1.clone.1 | convolution fusion | flops 200523776 | bytes 1497088 | tf_op jit(solution)/shard_map/while/body/eval_jaxpr/dot_general | solution.py:14
  81.1 1.0 dynamic-slice_bitcast_fusion.2
  82.2 1.4 %convolution_maximum_fusion.11 = f32[1024,256]{1,0:T(8,128)S(1)} fusion(bf16[256,256]{1,0:T(8,128)(2,1)S(1)} %get-tuple-element.215, bf16[124,256]{1,0:T(8,128)(2,1)} %get-tuple-element.214, bf16[512,124]{0,1:T(8,128)(2,1)S(1)} %get-tuple-element.181, bf16[512,124]{0,1:T(8,128)(2,1)S(1)} %get-tuple-element.182), kind=kOutput, calls=%fused_computation.1.clone.1 | convolution fusion | flops 200523776 | bytes 1497088 | tf_op jit(solution)/shard_map/while/body/eval_jaxpr/dot_general | solution.py:14
  86.0 7.5 %all_to_all.21 = f32[8,5,4,128]{3,2,1,0:T(4,128)S(1)} all-to-all(f32[8,5,4,128]{3,2,1,0:T(4,128)S(1)} %copy.42), channel_id=1, replica_groups=mesh['dp'=8,'mp'=4] {'dp'}, dimensions={0} | all-to-all | bytes 163840 | tf_op jit(solution)/shard_map/all_to_all | solution.py:80
  93.5 0.6 copy.43
  94.1 3.3 %all-to-all-start.3 = ((f32[8,5,4,128]{3,0,1,2:T(8,128)}), f32[8,5,4,128]{3,0,1,2:T(8,128)S(1)}, u32[]{:S(2)}, u32[]{:S(2)}) async-start(f32[8,5,4,128]{3,0,1,2:T(8,128)} %copy.43), calls=%async_computation.3 | async-start | bytes 163840 | tf_op jit(solution)/shard_map/all_to_all | solution.py:79
  97.8 5.4 %all-to-all-done.3 = f32[8,5,4,128]{3,0,1,2:T(8,128)S(1)} async-done(((f32[8,5,4,128]{3,0,1,2:T(8,128)}), f32[8,5,4,128]{3,0,1,2:T(8,128)S(1)}, u32[]{:S(2)}, u32[]{:S(2)}) %all-to-all-start.3) | async-done | bytes 81952 | tf_op jit(solution)/shard_map/all_to_all | solution.py:79
  103.9 0.6 fusion.55
  (138 shorter events, 21.5 us)
Async XLA Ops:
  0.6 24.6 %copy-start = (bf16[2048,256]{1,0:T(8,128)(2,1)S(1)}, bf16[2048,256]{1,0:T(8,128)(2,1)}, u32[]{:S(2)}) copy-start(bf16[2048,256]{1,0:T(8,128)(2,1)} %param.11) | copy-start | bytes 3145732
  14.8 10.5 %all-to-all-start.1 = ((s32[4,8,1,128]{3,1,2,0:T(8,128)}), s32[4,8,1,128]{3,1,2,0:T(8,128)S(1)}, u32[]{:S(2)}, u32[]{:S(2)}) async-start(s32[4,8,1,128]{3,1,2,0:T(8,128)} %pad_add_fusion), calls=%async_computation.1 | async-start | bytes 32768 | tf_op jit(solution)/shard_map/all_to_all | solution.py:9
  45.1 1.6 %copy-start.1 = (bf16[2,256]{1,0:T(2,128)(2,1)S(1)}, bf16[2,256]{1,0:T(2,128)(2,1)}, u32[]{:S(2)}) copy-start(bf16[2,256]{1,0:T(2,128)(2,1)} %param.16) | copy-start | bytes 3076
  45.1 1.6 %copy-start.5 = (bf16[256,256]{1,0:T(8,128)(2,1)S(1)}, bf16[256,256]{1,0:T(8,128)(2,1)}, u32[]{:S(2)}) copy-start(bf16[256,256]{1,0:T(8,128)(2,1)} %param.18) | copy-start | bytes 393220
  45.1 1.6 %copy-start.6 = (bf16[256]{0:T(256)(128)(2,1)S(1)}, bf16[256]{0:T(256)(128)(2,1)}, u32[]{:S(2)}) copy-start(bf16[256]{0:T(256)(128)(2,1)} %param.19) | copy-start | bytes 1540
  46.7 50.8 %copy-start.3 = (s32[1024,1]{0,1:T(1,128)S(1)}, s32[1024,1]{0,1:T(1,128)}, u32[]{:S(2)}) copy-start(s32[1024,1]{0,1:T(1,128)} %param.12) | copy-start | bytes 12292
  46.7 3.1 %copy-start.4 = (bf16[2,256,256]{2,1,0:T(8,128)(2,1)S(1)}, bf16[2,256,256]{2,1,0:T(8,128)(2,1)}, u32[]{:S(2)}) copy-start(bf16[2,256,256]{2,1,0:T(8,128)(2,1)} %get-tuple-element.212) | copy-start | bytes 786436 | tf_op jit(solution)/shard_map/while
  51.6 3.1 %copy-start.4 = (bf16[2,256,256]{2,1,0:T(8,128)(2,1)S(1)}, bf16[2,256,256]{2,1,0:T(8,128)(2,1)}, u32[]{:S(2)}) copy-start(bf16[2,256,256]{2,1,0:T(8,128)(2,1)} %get-tuple-element.212) | copy-start | bytes 786436 | tf_op jit(solution)/shard_map/while
  56.5 3.1 %copy-start.4 = (bf16[2,256,256]{2,1,0:T(8,128)(2,1)S(1)}, bf16[2,256,256]{2,1,0:T(8,128)(2,1)}, u32[]{:S(2)}) copy-start(bf16[2,256,256]{2,1,0:T(8,128)(2,1)} %get-tuple-element.212) | copy-start | bytes 786436 | tf_op jit(solution)/shard_map/while
  61.4 3.1 %copy-start.4 = (bf16[2,256,256]{2,1,0:T(8,128)(2,1)S(1)}, bf16[2,256,256]{2,1,0:T(8,128)(2,1)}, u32[]{:S(2)}) copy-start(bf16[2,256,256]{2,1,0:T(8,128)(2,1)} %get-tuple-element.212) | copy-start | bytes 786436 | tf_op jit(solution)/shard_map/while
  66.4 3.1 %copy-start.4 = (bf16[2,256,256]{2,1,0:T(8,128)(2,1)S(1)}, bf16[2,256,256]{2,1,0:T(8,128)(2,1)}, u32[]{:S(2)}) copy-start(bf16[2,256,256]{2,1,0:T(8,128)(2,1)} %get-tuple-element.212) | copy-start | bytes 786436 | tf_op jit(solution)/shard_map/while
  71.3 3.1 %copy-start.4 = (bf16[2,256,256]{2,1,0:T(8,128)(2,1)S(1)}, bf16[2,256,256]{2,1,0:T(8,128)(2,1)}, u32[]{:S(2)}) copy-start(bf16[2,256,256]{2,1,0:T(8,128)(2,1)} %get-tuple-element.212) | copy-start | bytes 786436 | tf_op jit(solution)/shard_map/while
  76.2 3.1 %copy-start.4 = (bf16[2,256,256]{2,1,0:T(8,128)(2,1)S(1)}, bf16[2,256,256]{2,1,0:T(8,128)(2,1)}, u32[]{:S(2)}) copy-start(bf16[2,256,256]{2,1,0:T(8,128)(2,1)} %get-tuple-element.212) | copy-start | bytes 786436 | tf_op jit(solution)/shard_map/while
  81.1 3.1 %copy-start.4 = (bf16[2,256,256]{2,1,0:T(8,128)(2,1)S(1)}, bf16[2,256,256]{2,1,0:T(8,128)(2,1)}, u32[]{:S(2)}) copy-start(bf16[2,256,256]{2,1,0:T(8,128)(2,1)} %get-tuple-element.212) | copy-start | bytes 786436 | tf_op jit(solution)/shard_map/while
  94.1 9.1 %all-to-all-start.3 = ((f32[8,5,4,128]{3,0,1,2:T(8,128)}), f32[8,5,4,128]{3,0,1,2:T(8,128)S(1)}, u32[]{:S(2)}, u32[]{:S(2)}) async-start(f32[8,5,4,128]{3,0,1,2:T(8,128)} %copy.43), calls=%async_computation.3 | async-start | bytes 163840 | tf_op jit(solution)/shard_map/all_to_all | solution.py:79
  103.8 1.2 %copy-start.2 = (f32[1,1024]{1,0:T(1,128)}, f32[1,1024]{1,0:T(1,128)S(1)}, u32[]{:S(2)}) copy-start(f32[1,1024]{1,0:T(1,128)S(1)} %get-tuple-element.108) | copy-start | bytes 12292
